TPU v7x, 512 devices: a whole 4x8x8 slice. The times are simulated.
512 devices in a mesh: group: 8 (over y), mesh: 32 (over z, x), comp: 2 (over core).
Axes of the slice: x: 4, y: 8, z: 8, core: 2. Of those that a mesh axis runs over, the one named last changes fastest.
Arguments:
- log_sigma: float32 [2048, 128], P('mesh'), may hold values from -1 to 1
- block_owner: int32 [8, 4096, 1], P('group', 'mesh'), may hold values from 0 to 31; in each aligned block of 128 rows (0 to 127, 128 to 255, ..., all dimensions but the last counted through in order) at most 8 rows name the same one
- block_slot: int32 [8, 4096], P('group', 'mesh'), may hold values from 0 to 63
- coupling: float32 [128, 128], replicated, may hold values from -0.6 to 10, as said below
- sources: float32 [8, 2, 8, 4096, 128], P('group', 'comp', None, 'mesh'), may hold values from -24 to 24
- rcv_cell: int32 [8, 4096], P('group', 'mesh'), may hold values from 0 to 16383
- observed: float32 [8, 2, 8, 4096], P('group', 'comp', None, 'mesh'), may hold values from -6 to 6
Outputs:
- gradient: float32 [2048, 128], P('mesh')
Inputs may be any that keep to these rules, and one draw needn't show every extreme that they name: `block_owner`: in the 128 rows of one device of a group, no owner is named more than 8 times; some owner is named exactly 8 times in some device's rows. `rcv_cell`: A receiver's cell counts from the first cell of the modelling section of the device that holds the receiver's entry. `coupling`: every diagonal entry is 6 or more.
All inputs are finite; a program needn't handle non-finite values.
Results may differ from a plain program's by a relative error of at most 0.0003.
Values sent between devices are 32-bit elements; how exact they have to be, the bound alone decides.
A program may use at most 64 MiB of HBM per device.

v0:
```python
import jax
import jax.numpy as jnp
from jax import lax
from jax.sharding import PartitionSpec as P

CELLS = 128
S = 8
ITERS = 6
omega_freq = 0.8
chain_weight = 1.0


def from_partner(value, axis, distance):
    mask = 2**distance
    pairs = [(source, source ^ mask) for source in range(lax.axis_size(axis))]
    return lax.ppermute(value, axis, pairs)


def with_halo(x, sides, width):
    for axis, dim in sides:
        size, length = (lax.axis_size(axis), x.shape[dim])
        up = [(i, (i + 1) % size) for i in range(size - 1)]
        down = [(j, i) for i, j in up]
        last = lax.slice_in_dim(x, length - width, length, axis=dim)
        initial = lax.slice_in_dim(x, 0, width, axis=dim)
        before = lax.ppermute(last, axis, up)
        after = lax.ppermute(initial, axis, down)
        x = jnp.concatenate([before, x, after], axis=dim)
    return x


def partner(values):
    return from_partner(values, "comp", 0)


def beside(values):
    padded = with_halo(values, (("mesh", 1),), 1)
    return padded[:, :-2] + padded[:, 2:]


def cell_product(values, matrix):
    shaped = values.reshape(values.shape[:-1] + (-1, CELLS))
    product = jnp.einsum("...bj,ij->...bi", shaped, matrix, precision=lax.Precision.HIGHEST)
    return product.reshape(values.shape)


def operate(values, matrix, cross_coef):
    return (
        cell_product(values, matrix) - chain_weight * beside(values) + cross_coef * partner(values)
    )


def relax(right, matrix, cross_coef, inverse_diag, apply_op):
    state = jnp.zeros_like(right)
    for iteration in range(ITERS):
        state = state + inverse_diag * (right - apply_op(state, matrix, cross_coef))
    return state


def local(log_sigma, block_owner, block_slot, coupling, sources, rcv_cell, observed):
    owners = block_owner[0, :, 0]
    slots = block_slot[0]
    blocks_dev = owners.shape[0]
    inv_rows = log_sigma.shape[0]
    targets = owners * inv_rows + slots
    gathered = lax.all_gather(log_sigma, "mesh", axis=0, tiled=True)
    model_part = jnp.take(gathered, targets, axis=0)
    sigmas = jnp.exp(model_part).reshape(-1)
    receivers = rcv_cell[0]
    parity = (2 * lax.axis_index("comp") - 1).astype(jnp.float32)
    forward_coef = parity * omega_freq * sigmas
    inverse_diag = jnp.tile(1.0 / jnp.diagonal(coupling), blocks_dev)
    right = sources.reshape(S, -1)
    field_now = relax(right, coupling, forward_coef, inverse_diag, operate)
    field_other = partner(field_now)
    misfit = field_now[:, receivers] - observed[0, 0]
    adjoint_src = jnp.zeros_like(right).at[:, receivers].add(misfit)
    adjoint = relax(adjoint_src, coupling.T, -forward_coef, inverse_diag, operate)
    weighted = -parity * jnp.sum(adjoint * field_other, axis=0)
    partial_rows = (omega_freq * sigmas * weighted).reshape(blocks_dev, CELLS)
    inside_rows = (targets >= 0) & (targets < inv_rows * lax.axis_size("mesh"))
    kept_rows = jnp.where(inside_rows, targets, inv_rows * lax.axis_size("mesh"))
    owned = lax.psum_scatter(
        jnp.zeros((inv_rows * lax.axis_size("mesh"), CELLS), jnp.float32)
        .at[kept_rows]
        .add(partial_rows, mode="drop"),
        "mesh",
        scatter_dimension=0,
        tiled=True,
    )
    return lax.psum(owned, ("group", "comp"))


def solution(mesh):
    in_specs = (
        P("mesh", None),
        P("group", "mesh", None),
        P("group", "mesh"),
        P(),
        P("group", "comp", None, "mesh", None),
        P("group", "mesh"),
        P("group", "comp", None, "mesh"),
    )
    out_specs = P("mesh", None)
    return jax.shard_map(local, mesh=mesh, in_specs=in_specs, out_specs=out_specs, check_vma=False)
```

profile of v0, /device:TPU:32, one launch (start us, length us, event | category | flops | bytes accessed | tf_op | source)
XLA Modules:
  0.0 532.8 jit_solution(2460921501740615536)
XLA Ops:
  7.3 1.3 collective-permute-start.1
  8.6 4.5 collective-permute-start
  13.2 1.9 collective-permute-start.2
  18.4 78.7 %all-gather.2.cloned.1.call-done = f32[2048,128]{1,0:T(8,128)} async-done(((f32[64,128]{1,0:T(8,128)}), f32[2048,128]{1,0:T(8,128)}) %all-gather.2.cloned.1.call-update) | async-done | bytes 1048592 | tf_op jit(solution)/shard_map/all_gather | solution.py:66
  97.1 1.9 gather_fusion
  99.1 1.7 fusion.8
  100.8 1.9 collective-permute-start.5
  102.8 1.3 collective-permute-start.4
  104.1 4.5 collective-permute-start.3
  108.6 1.3 collective-permute-done.3
  109.9 1.9 fusion.10
  111.9 1.9 collective-permute-start.8
  113.9 1.3 collective-permute-start.7
  115.2 4.8 collective-permute-start.6
  121.8 1.9 collective-permute-start.11
  123.8 1.3 collective-permute-start.10
  125.1 4.8 collective-permute-start.9
  129.9 1.3 collective-permute-done.9
  132.1 1.9 collective-permute-start.14
  134.1 1.3 collective-permute-start.13
  135.4 4.8 collective-permute-start.12
  142.1 1.9 collective-permute-start.17
  144.8 1.3 collective-permute-start.16
  146.1 5.5 %collective-permute-start.15 = (f32[8,1]{1,0:T(8,128)S(1)}, f32[8,1]{1,0:T(8,128)S(1)}, u32[]{:S(2)}, u32[]{:S(2)}) collective-permute-start(f32[8,1]{1,0:T(8,128)S(1)} %get-tuple-element.17), channel_id=1, source_target_pairs={{0,2},{2,4},{4,6},{6,8},{8,10},{10,12},{12,14},{14,16},{16,18},{18... | collective-permute-start | bytes 104 | tf_op jit(solution)/shard_map/ppermute | solution.py:26
  151.6 1.3 collective-permute-done.15
  152.9 1.9 fusion.18
  154.8 5.3 copy.271
  160.1 6.0 %scatter_custom_fusion = f32[8,16384]{0,1:T(8,128)} fusion(s32[128]{0:T(128)S(1)} %fusion.122, f32[]{:T(128)} %constant.12.clone.1, f32[1,1,8,128]{2,3,1,0:T(8,128)S(1)} %copy.272, f32[8,16384]{0,1:T(8,128)} %copy.271, s32[1024]{0:T(1024)S(1)} %pad_clamp_fusion), kind=kCustom, calls=%fused_computation.15 | custom fusion | flops 2048 | bytes 1118212 | tf_op jit(solution)/shard_map/scatter-add | solution.py:77
  166.1 5.5 %copy.273 = f32[8,16384]{1,0:T(8,128)S(1)} copy(f32[8,16384]{0,1:T(8,128)} %scatter_custom_fusion) | data formatting | bytes 1048576 | tf_op jit(solution)/shard_map/scatter-add | solution.py:77
  172.0 1.9 collective-permute-start.20
  174.0 1.3 collective-permute-start.19
  175.3 6.9 %collective-permute-start.18 = (f32[8,1]{1,0:T(8,128)S(1)}, f32[8,1]{1,0:T(8,128)S(1)}, u32[]{:S(2)}, u32[]{:S(2)}) collective-permute-start(f32[8,1]{1,0:T(8,128)S(1)} %get-tuple-element.15), channel_id=1, source_target_pairs={{0,2},{2,4},{4,6},{6,8},{8,10},{10,12},{12,14},{14,16},{16,18},{18... | collective-permute-start | bytes 104 | tf_op jit(solution)/shard_map/ppermute | solution.py:26
  182.3 1.3 collective-permute-done.18
  184.2 1.9 collective-permute-start.23
  186.2 1.3 collective-permute-start.22
  187.5 6.9 %collective-permute-start.21 = (f32[8,1]{1,0:T(8,128)S(1)}, f32[8,1]{1,0:T(8,128)S(1)}, u32[]{:S(2)}, u32[]{:S(2)}) collective-permute-start(f32[8,1]{1,0:T(8,128)S(1)} %get-tuple-element.13), channel_id=1, source_target_pairs={{0,2},{2,4},{4,6},{6,8},{8,10},{10,12},{12,14},{14,16},{16,18},{18... | collective-permute-start | bytes 104 | tf_op jit(solution)/shard_map/ppermute | solution.py:26
  196.2 1.9 collective-permute-start.26
  199.5 6.9 %collective-permute-start.24 = (f32[8,1]{1,0:T(8,128)S(1)}, f32[8,1]{1,0:T(8,128)S(1)}, u32[]{:S(2)}, u32[]{:S(2)}) collective-permute-start(f32[8,1]{1,0:T(8,128)S(1)} %get-tuple-element.11), channel_id=1, source_target_pairs={{0,2},{2,4},{4,6},{6,8},{8,10},{10,12},{12,14},{14,16},{16,18},{18... | collective-permute-start | bytes 104 | tf_op jit(solution)/shard_map/ppermute | solution.py:26
  206.4 1.3 collective-permute-done.24
  208.4 1.9 collective-permute-start.29
  210.3 2.4 collective-permute-start.33
  214.1 6.9 %collective-permute-start.27 = (f32[8,1]{1,0:T(8,128)S(1)}, f32[8,1]{1,0:T(8,128)S(1)}, u32[]{:S(2)}, u32[]{:S(2)}) collective-permute-start(f32[8,1]{1,0:T(8,128)S(1)} %get-tuple-element.9), channel_id=1, source_target_pairs={{0,2},{2,4},{4,6},{6,8},{8,10},{10,12},{12,14},{14,16},{16,18},{18... | collective-permute-start | bytes 104 | tf_op jit(solution)/shard_map/ppermute | solution.py:26
  222.8 1.9 collective-permute-start.32
  224.8 1.3 collective-permute-start.31
  226.1 6.9 %collective-permute-start.30 = (f32[8,1]{1,0:T(8,128)S(1)}, f32[8,1]{1,0:T(8,128)S(1)}, u32[]{:S(2)}, u32[]{:S(2)}) collective-permute-start(f32[8,1]{1,0:T(8,128)S(1)} %get-tuple-element.7), channel_id=1, source_target_pairs={{0,2},{2,4},{4,6},{6,8},{8,10},{10,12},{12,14},{14,16},{16,18},{18... | collective-permute-start | bytes 104 | tf_op jit(solution)/shard_map/ppermute | solution.py:26
  234.7 2.1 scatter_custom_fusion.1
  236.8 242.3 %reduce-scatter.2.cloned.1.call-done = f32[64,128]{1,0:T(8,128)} async-done(((f32[2048,128]{1,0:T(8,128)}), f32[64,128]{1,0:T(8,128)}) %reduce-scatter.2.cloned.1.call-update) | async-done | bytes 32784 | tf_op jit(solution)/shard_map/reduce_scatter | solution.py:83
  479.1 46.9 %psum.7 = f32[64,128]{1,0:T(8,128)} all-reduce(f32[64,128]{1,0:T(8,128)} %reduce-scatter.2.cloned.1.call-done), channel_id=1, replica_groups=mesh['group'=8,'mesh'=32,'comp'=2] {'group','comp'}, use_global_device_ids=true, to_apply=%region_4.5 | all-reduce | flops 8192 | bytes 65536 | tf_op jit(solution)/shard_map/psum | solution.py:91
  (82 shorter events, 19.5 us)
Async XLA Ops:
  6.5 8.7 %copy-start = (f32[128,128]{1,0:T(8,128)S(1)}, f32[128,128]{1,0:T(8,128)}, u32[]{:S(2)}) copy-start(f32[128,128]{1,0:T(8,128)} %param.10) | copy-start | bytes 196612
  6.5 114.8 %copy-start.1 = (f32[1,1,8,128,128]{4,3,2,1,0:T(8,128)S(1)}, f32[1,1,8,128,128]{4,3,2,1,0:T(8,128)}, u32[]{:S(2)}) copy-start(f32[1,1,8,128,128]{4,3,2,1,0:T(8,128)} %param.11) | copy-start | bytes 1572868
  6.5 90.6 %all-gather.2.cloned.1.call-start = ((), (), s32[]{:S(2)}) async-start(), calls=%async_computation.1 | async-start | bytes 1081344 | tf_op jit(solution)/shard_map/all_gather | solution.py:66
  7.3 471.8 %reduce-scatter.2.cloned.1.call-start = ((), (), s32[]{:S(2)}) async-start(), calls=%async_computation.2 | async-start | bytes 1081344 | tf_op jit(solution)/shard_map/reduce_scatter | solution.py:83
  7.3 91.8 %collective-permute-start.1 = (f32[8,1]{1,0:T(8,128)S(1)}, f32[8,1]{1,0:T(8,128)S(1)}, u32[]{:S(2)}, u32[]{:S(2)}) collective-permute-start(f32[8,1]{1,0:T(8,128)S(1)} %broadcast.157), channel_id=1, source_target_pairs={{2,0},{4,2},{6,4},{8,6},{10,8},{12,10},{14,12},{16,14},{18,16},{20... | collective-permute-start | bytes 104 | tf_op jit(solution)/shard_map/ppermute | solution.py:27
  8.6 90.5 %collective-permute-start = (f32[8,1]{1,0:T(8,128)S(1)}, f32[8,1]{1,0:T(8,128)S(1)}, u32[]{:S(2)}, u32[]{:S(2)}) collective-permute-start(f32[8,1]{1,0:T(8,128)S(1)} %broadcast.157), channel_id=1, source_target_pairs={{0,2},{2,4},{4,6},{6,8},{8,10},{10,12},{12,14},{14,16},{16,18},{18... | collective-permute-start | bytes 104 | tf_op jit(solution)/shard_map/ppermute | solution.py:26
  13.2 130.8 %copy-start.3 = (s32[1,128]{1,0:T(1,128)S(1)}, s32[1,128]{1,0:T(1,128)}, u32[]{:S(2)}) copy-start(s32[1,128]{1,0:T(1,128)} %param.12) | copy-start | bytes 1540
  13.2 130.8 %copy-start.2 = (f32[1,1,8,128]{3,2,1,0:T(8,128)S(1)}, f32[1,1,8,128]{3,2,1,0:T(8,128)}, u32[]{:S(2)}) copy-start(f32[1,1,8,128]{3,2,1,0:T(8,128)} %param.13) | copy-start | bytes 12292
  13.2 85.8 %collective-permute-start.2 = (f32[8,16384]{1,0:T(8,128)S(1)}, f32[8,16384]{1,0:T(8,128)S(1)}, u32[]{:S(2)}, u32[]{:S(2)}) collective-permute-start(f32[8,16384]{1,0:T(8,128)S(1)} %broadcast.154.clone), channel_id=1, source_target_pairs={{0,1},{1,0},{2,3},{3,2},{4,5},{5,4},{6,7},{7,6},{8,9},{9,8},{10,11... | collective-permute-start | bytes 1572872 | tf_op jit(solution)/shard_map/ppermute | solution.py:16
  100.8 9.2 %collective-permute-start.5 = (f32[8,16384]{1,0:T(8,128)S(1)}, f32[8,16384]{1,0:T(8,128)S(1)}, u32[]{:S(2)}, u32[]{:S(2)}) collective-permute-start(f32[8,16384]{1,0:T(8,128)S(1)} %fusion.8), channel_id=1, source_target_pairs={{0,1},{1,0},{2,3},{3,2},{4,5},{5,4},{6,7},{7,6},{8,9},{9,8},{10,11... | collective-permute-start | bytes 1572872 | tf_op jit(solution)/shard_map/ppermute | solution.py:16
  102.8 5.8 %collective-permute-start.4 = (f32[8,1]{1,0:T(8,128)S(1)}, f32[8,1]{1,0:T(8,128)S(1)}, u32[]{:S(2)}, u32[]{:S(2)}) collective-permute-start(f32[8,1]{1,0:T(8,128)S(1)} %get-tuple-element.26), channel_id=1, source_target_pairs={{2,0},{4,2},{6,4},{8,6},{10,8},{12,10},{14,12},{16,14},{18,16},{20... | collective-permute-start | bytes 104 | tf_op jit(solution)/shard_map/ppermute | solution.py:27
  104.1 5.9 %collective-permute-start.3 = (f32[8,1]{1,0:T(8,128)S(1)}, f32[8,1]{1,0:T(8,128)S(1)}, u32[]{:S(2)}, u32[]{:S(2)}) collective-permute-start(f32[8,1]{1,0:T(8,128)S(1)} %get-tuple-element.25), channel_id=1, source_target_pairs={{0,2},{2,4},{4,6},{6,8},{8,10},{10,12},{12,14},{14,16},{16,18},{18... | collective-permute-start | bytes 104 | tf_op jit(solution)/shard_map/ppermute | solution.py:26
  111.9 9.4 %collective-permute-start.8 = (f32[8,16384]{1,0:T(8,128)S(1)}, f32[8,16384]{1,0:T(8,128)S(1)}, u32[]{:S(2)}, u32[]{:S(2)}) collective-permute-start(f32[8,16384]{1,0:T(8,128)S(1)} %fusion.10), channel_id=1, source_target_pairs={{0,1},{1,0},{2,3},{3,2},{4,5},{5,4},{6,7},{7,6},{8,9},{9,8},{10,11... | collective-permute-start | bytes 1572872 | tf_op jit(solution)/shard_map/ppermute | solution.py:16
  113.9 6.7 %collective-permute-start.7 = (f32[8,1]{1,0:T(8,128)S(1)}, f32[8,1]{1,0:T(8,128)S(1)}, u32[]{:S(2)}, u32[]{:S(2)}) collective-permute-start(f32[8,1]{1,0:T(8,128)S(1)} %get-tuple-element.24), channel_id=1, source_target_pairs={{2,0},{4,2},{6,4},{8,6},{10,8},{12,10},{14,12},{16,14},{18,16},{20... | collective-permute-start | bytes 104 | tf_op jit(solution)/shard_map/ppermute | solution.py:27
  115.2 6.1 %collective-permute-start.6 = (f32[8,1]{1,0:T(8,128)S(1)}, f32[8,1]{1,0:T(8,128)S(1)}, u32[]{:S(2)}, u32[]{:S(2)}) collective-permute-start(f32[8,1]{1,0:T(8,128)S(1)} %get-tuple-element.23), channel_id=1, source_target_pairs={{0,2},{2,4},{4,6},{6,8},{8,10},{10,12},{12,14},{14,16},{16,18},{18... | collective-permute-start | bytes 104 | tf_op jit(solution)/shard_map/ppermute | solution.py:26
  121.8 9.4 %collective-permute-start.11 = (f32[8,16384]{1,0:T(8,128)S(1)}, f32[8,16384]{1,0:T(8,128)S(1)}, u32[]{:S(2)}, u32[]{:S(2)}) collective-permute-start(f32[8,16384]{1,0:T(8,128)S(1)} %fusion.12), channel_id=1, source_target_pairs={{0,1},{1,0},{2,3},{3,2},{4,5},{5,4},{6,7},{7,6},{8,9},{9,8},{10,11... | collective-permute-start | bytes 1572872 | tf_op jit(solution)/shard_map/ppermute | solution.py:16
  123.8 6.1 %collective-permute-start.10 = (f32[8,1]{1,0:T(8,128)S(1)}, f32[8,1]{1,0:T(8,128)S(1)}, u32[]{:S(2)}, u32[]{:S(2)}) collective-permute-start(f32[8,1]{1,0:T(8,128)S(1)} %get-tuple-element.22), channel_id=1, source_target_pairs={{2,0},{4,2},{6,4},{8,6},{10,8},{12,10},{14,12},{16,14},{18,16},{20... | collective-permute-start | bytes 104 | tf_op jit(solution)/shard_map/ppermute | solution.py:27
  125.1 6.1 %collective-permute-start.9 = (f32[8,1]{1,0:T(8,128)S(1)}, f32[8,1]{1,0:T(8,128)S(1)}, u32[]{:S(2)}, u32[]{:S(2)}) collective-permute-start(f32[8,1]{1,0:T(8,128)S(1)} %get-tuple-element.21), channel_id=1, source_target_pairs={{0,2},{2,4},{4,6},{6,8},{8,10},{10,12},{12,14},{14,16},{16,18},{18... | collective-permute-start | bytes 104 | tf_op jit(solution)/shard_map/ppermute | solution.py:26
  132.1 9.4 %collective-permute-start.14 = (f32[8,16384]{1,0:T(8,128)S(1)}, f32[8,16384]{1,0:T(8,128)S(1)}, u32[]{:S(2)}, u32[]{:S(2)}) collective-permute-start(f32[8,16384]{1,0:T(8,128)S(1)} %fusion.14), channel_id=1, source_target_pairs={{0,1},{1,0},{2,3},{3,2},{4,5},{5,4},{6,7},{7,6},{8,9},{9,8},{10,11... | collective-permute-start | bytes 1572872 | tf_op jit(solution)/shard_map/ppermute | solution.py:16
  134.1 6.7 %collective-permute-start.13 = (f32[8,1]{1,0:T(8,128)S(1)}, f32[8,1]{1,0:T(8,128)S(1)}, u32[]{:S(2)}, u32[]{:S(2)}) collective-permute-start(f32[8,1]{1,0:T(8,128)S(1)} %get-tuple-element.20), channel_id=1, source_target_pairs={{2,0},{4,2},{6,4},{8,6},{10,8},{12,10},{14,12},{16,14},{18,16},{20... | collective-permute-start | bytes 104 | tf_op jit(solution)/shard_map/ppermute | solution.py:27
  135.4 6.1 %collective-permute-start.12 = (f32[8,1]{1,0:T(8,128)S(1)}, f32[8,1]{1,0:T(8,128)S(1)}, u32[]{:S(2)}, u32[]{:S(2)}) collective-permute-start(f32[8,1]{1,0:T(8,128)S(1)} %get-tuple-element.19), channel_id=1, source_target_pairs={{0,2},{2,4},{4,6},{6,8},{8,10},{10,12},{12,14},{14,16},{16,18},{18... | collective-permute-start | bytes 104 | tf_op jit(solution)/shard_map/ppermute | solution.py:26
  142.1 10.8 %collective-permute-start.17 = (f32[8,16384]{1,0:T(8,128)S(1)}, f32[8,16384]{1,0:T(8,128)}, u32[]{:S(2)}, u32[]{:S(2)}) collective-permute-start(f32[8,16384]{1,0:T(8,128)S(1)} %fusion.16), channel_id=1, source_target_pairs={{0,1},{1,0},{2,3},{3,2},{4,5},{5,4},{6,7},{7,6},{8,9},{9,8},{10,11... | collective-permute-start | bytes 1572872 | tf_op jit(solution)/shard_map/ppermute | solution.py:16
  144.8 6.8 %collective-permute-start.16 = (f32[8,1]{1,0:T(8,128)S(1)}, f32[8,1]{1,0:T(8,128)S(1)}, u32[]{:S(2)}, u32[]{:S(2)}) collective-permute-start(f32[8,1]{1,0:T(8,128)S(1)} %get-tuple-element.18), channel_id=1, source_target_pairs={{2,0},{4,2},{6,4},{8,6},{10,8},{12,10},{14,12},{16,14},{18,16},{20... | collective-permute-start | bytes 104 | tf_op jit(solution)/shard_map/ppermute | solution.py:27
  146.1 6.8 %collective-permute-start.15 = (f32[8,1]{1,0:T(8,128)S(1)}, f32[8,1]{1,0:T(8,128)S(1)}, u32[]{:S(2)}, u32[]{:S(2)}) collective-permute-start(f32[8,1]{1,0:T(8,128)S(1)} %get-tuple-element.17), channel_id=1, source_target_pairs={{0,2},{2,4},{4,6},{6,8},{8,10},{10,12},{12,14},{14,16},{16,18},{18... | collective-permute-start | bytes 104 | tf_op jit(solution)/shard_map/ppermute | solution.py:26
  172.0 11.5 %collective-permute-start.20 = (f32[8,16384]{1,0:T(8,128)S(1)}, f32[8,16384]{1,0:T(8,128)S(1)}, u32[]{:S(2)}, u32[]{:S(2)}) collective-permute-start(f32[8,16384]{1,0:T(8,128)S(1)} %fusion.5), channel_id=1, source_target_pairs={{0,1},{1,0},{2,3},{3,2},{4,5},{5,4},{6,7},{7,6},{8,9},{9,8},{10,11... | collective-permute-start | bytes 1572872 | tf_op jit(solution)/shard_map/ppermute | solution.py:16
  174.0 8.2 %collective-permute-start.19 = (f32[8,1]{1,0:T(8,128)S(1)}, f32[8,1]{1,0:T(8,128)S(1)}, u32[]{:S(2)}, u32[]{:S(2)}) collective-permute-start(f32[8,1]{1,0:T(8,128)S(1)} %get-tuple-element.16), channel_id=1, source_target_pairs={{2,0},{4,2},{6,4},{8,6},{10,8},{12,10},{14,12},{16,14},{18,16},{20... | collective-permute-start | bytes 104 | tf_op jit(solution)/shard_map/ppermute | solution.py:27
  175.3 8.3 %collective-permute-start.18 = (f32[8,1]{1,0:T(8,128)S(1)}, f32[8,1]{1,0:T(8,128)S(1)}, u32[]{:S(2)}, u32[]{:S(2)}) collective-permute-start(f32[8,1]{1,0:T(8,128)S(1)} %get-tuple-element.15), channel_id=1, source_target_pairs={{0,2},{2,4},{4,6},{6,8},{8,10},{10,12},{12,14},{14,16},{16,18},{18... | collective-permute-start | bytes 104 | tf_op jit(solution)/shard_map/ppermute | solution.py:26
  184.2 11.5 %collective-permute-start.23 = (f32[8,16384]{1,0:T(8,128)S(1)}, f32[8,16384]{1,0:T(8,128)S(1)}, u32[]{:S(2)}, u32[]{:S(2)}) collective-permute-start(f32[8,16384]{1,0:T(8,128)S(1)} %fusion.50), channel_id=1, source_target_pairs={{0,1},{1,0},{2,3},{3,2},{4,5},{5,4},{6,7},{7,6},{8,9},{9,8},{10,11... | collective-permute-start | bytes 1572872 | tf_op jit(solution)/shard_map/ppermute | solution.py:16
  186.2 8.8 %collective-permute-start.22 = (f32[8,1]{1,0:T(8,128)S(1)}, f32[8,1]{1,0:T(8,128)S(1)}, u32[]{:S(2)}, u32[]{:S(2)}) collective-permute-start(f32[8,1]{1,0:T(8,128)S(1)} %get-tuple-element.14), channel_id=1, source_target_pairs={{2,0},{4,2},{6,4},{8,6},{10,8},{12,10},{14,12},{16,14},{18,16},{20... | collective-permute-start | bytes 104 | tf_op jit(solution)/shard_map/ppermute | solution.py:27
  187.5 8.2 %collective-permute-start.21 = (f32[8,1]{1,0:T(8,128)S(1)}, f32[8,1]{1,0:T(8,128)S(1)}, u32[]{:S(2)}, u32[]{:S(2)}) collective-permute-start(f32[8,1]{1,0:T(8,128)S(1)} %get-tuple-element.13), channel_id=1, source_target_pairs={{0,2},{2,4},{4,6},{6,8},{8,10},{10,12},{12,14},{14,16},{16,18},{18... | collective-permute-start | bytes 104 | tf_op jit(solution)/shard_map/ppermute | solution.py:26
  196.2 11.5 %collective-permute-start.26 = (f32[8,16384]{1,0:T(8,128)S(1)}, f32[8,16384]{1,0:T(8,128)S(1)}, u32[]{:S(2)}, u32[]{:S(2)}) collective-permute-start(f32[8,16384]{1,0:T(8,128)S(1)} %fusion.44), channel_id=1, source_target_pairs={{0,1},{1,0},{2,3},{3,2},{4,5},{5,4},{6,7},{7,6},{8,9},{9,8},{10,11... | collective-permute-start | bytes 1572872 | tf_op jit(solution)/shard_map/ppermute | solution.py:16
  198.2 8.2 %collective-permute-start.25 = (f32[8,1]{1,0:T(8,128)S(1)}, f32[8,1]{1,0:T(8,128)S(1)}, u32[]{:S(2)}, u32[]{:S(2)}) collective-permute-start(f32[8,1]{1,0:T(8,128)S(1)} %get-tuple-element.12), channel_id=1, source_target_pairs={{2,0},{4,2},{6,4},{8,6},{10,8},{12,10},{14,12},{16,14},{18,16},{20... | collective-permute-start | bytes 104 | tf_op jit(solution)/shard_map/ppermute | solution.py:27
  199.5 8.2 %collective-permute-start.24 = (f32[8,1]{1,0:T(8,128)S(1)}, f32[8,1]{1,0:T(8,128)S(1)}, u32[]{:S(2)}, u32[]{:S(2)}) collective-permute-start(f32[8,1]{1,0:T(8,128)S(1)} %get-tuple-element.11), channel_id=1, source_target_pairs={{0,2},{2,4},{4,6},{6,8},{8,10},{10,12},{12,14},{14,16},{16,18},{18... | collective-permute-start | bytes 104 | tf_op jit(solution)/shard_map/ppermute | solution.py:26
  208.4 14.0 %collective-permute-start.29 = (f32[8,16384]{1,0:T(8,128)S(1)}, f32[8,16384]{1,0:T(8,128)S(1)}, u32[]{:S(2)}, u32[]{:S(2)}) collective-permute-start(f32[8,16384]{1,0:T(8,128)S(1)} %fusion.38), channel_id=1, source_target_pairs={{0,1},{1,0},{2,3},{3,2},{4,5},{5,4},{6,7},{7,6},{8,9},{9,8},{10,11... | collective-permute-start | bytes 1572872 | tf_op jit(solution)/shard_map/ppermute | solution.py:16
  210.3 23.2 %collective-permute-start.33 = (f32[8,16384]{1,0:T(8,128)S(1)}, f32[8,16384]{1,0:T(8,128)S(1)}, u32[]{:S(2)}, u32[]{:S(2)}) collective-permute-start(f32[8,16384]{1,0:T(8,128)S(1)} %fusion.18), channel_id=1, source_target_pairs={{0,1},{1,0},{2,3},{3,2},{4,5},{5,4},{6,7},{7,6},{8,9},{9,8},{10,11... | collective-permute-start | bytes 1572872 | tf_op jit(solution)/shard_map/ppermute | solution.py:16
  212.8 8.8 %collective-permute-start.28 = (f32[8,1]{1,0:T(8,128)S(1)}, f32[8,1]{1,0:T(8,128)S(1)}, u32[]{:S(2)}, u32[]{:S(2)}) collective-permute-start(f32[8,1]{1,0:T(8,128)S(1)} %get-tuple-element.10), channel_id=1, source_target_pairs={{2,0},{4,2},{6,4},{8,6},{10,8},{12,10},{14,12},{16,14},{18,16},{20... | collective-permute-start | bytes 104 | tf_op jit(solution)/shard_map/ppermute | solution.py:27
  214.1 8.3 %collective-permute-start.27 = (f32[8,1]{1,0:T(8,128)S(1)}, f32[8,1]{1,0:T(8,128)S(1)}, u32[]{:S(2)}, u32[]{:S(2)}) collective-permute-start(f32[8,1]{1,0:T(8,128)S(1)} %get-tuple-element.9), channel_id=1, source_target_pairs={{0,2},{2,4},{4,6},{6,8},{8,10},{10,12},{12,14},{14,16},{16,18},{18... | collective-permute-start | bytes 104 | tf_op jit(solution)/shard_map/ppermute | solution.py:26
  222.8 11.5 %collective-permute-start.32 = (f32[8,16384]{1,0:T(8,128)S(1)}, f32[8,16384]{1,0:T(8,128)S(1)}, u32[]{:S(2)}, u32[]{:S(2)}) collective-permute-start(f32[8,16384]{1,0:T(8,128)S(1)} %fusion.32), channel_id=1, source_target_pairs={{0,1},{1,0},{2,3},{3,2},{4,5},{5,4},{6,7},{7,6},{8,9},{9,8},{10,11... | collective-permute-start | bytes 1572872 | tf_op jit(solution)/shard_map/ppermute | solution.py:16
  224.8 8.8 %collective-permute-start.31 = (f32[8,1]{1,0:T(8,128)S(1)}, f32[8,1]{1,0:T(8,128)S(1)}, u32[]{:S(2)}, u32[]{:S(2)}) collective-permute-start(f32[8,1]{1,0:T(8,128)S(1)} %get-tuple-element.8), channel_id=1, source_target_pairs={{2,0},{4,2},{6,4},{8,6},{10,8},{12,10},{14,12},{16,14},{18,16},{20... | collective-permute-start | bytes 104 | tf_op jit(solution)/shard_map/ppermute | solution.py:27
  226.1 8.2 %collective-permute-start.30 = (f32[8,1]{1,0:T(8,128)S(1)}, f32[8,1]{1,0:T(8,128)S(1)}, u32[]{:S(2)}, u32[]{:S(2)}) collective-permute-start(f32[8,1]{1,0:T(8,128)S(1)} %get-tuple-element.7), channel_id=1, source_target_pairs={{0,2},{2,4},{4,6},{6,8},{8,10},{10,12},{12,14},{14,16},{16,18},{18... | collective-permute-start | bytes 104 | tf_op jit(solution)/shard_map/ppermute | solution.py:26
Sparse Core Ops, SparseCore 0:
  10.5 86.5 all-gather.1
  237.0 242.0 reduce-scatter.1
where the time goes:
time: 534 us; the launch traced here: 533 us
  waiting for transfers between devices  332 us (62%)
  starting transfers between devices  101 us (19%)
  blocking collectives  46.9 us (9%)
  local copies, waits for them, and re-layouts  14.9 us (3%)
  between operations  14 us (3%)
  other arithmetic  13.9 us (3%)
  matrix products  10.1 us (2%)
    reduce_scatter x1, waiting for transfers between devices, local(): lax.psum_scatter(jnp.zeros((inv_rows * lax.axis_size('mesh'), CELLS), jnp...  242 us
    all_gather x1, waiting for transfers between devices, local(): gathered = lax.all_gather(log_sigma, 'mesh', axis=0, tiled=True)  78.7 us
    ppermute x11, starting transfers between devices, with_halo(): before = lax.ppermute(last, axis, up)  63.6 us
    psum x1, blocking collectives, local(): return lax.psum(owned, ('group', 'comp'))  46.9 us
    ppermute x12, starting transfers between devices, from_partner(): return lax.ppermute(value, axis, pairs)  23.5 us
    ppermute x11, starting transfers between devices, with_halo(): after = lax.ppermute(initial, axis, down)  14.1 us
  transfers between devices with their start and end apart: 36, of which 12 were waited for; matrix products, arithmetic and copies ran while one was open for 2% of the time, Pallas kernels for 0%

commit v1 on v0

--- a/solution.py
+++ b/solution.py
@@ -88,7 +88,7 @@
         scatter_dimension=0,
         tiled=True,
     )
-    return lax.psum(owned, ("group", "comp"))
+    return jnp.sum(lax.all_gather(owned, ("group", "comp")), axis=0)
 
 
 def solution(mesh):

time: 534 us -> 508 us (0.951)
  the two profiles are of different devices: /device:TPU:32 before, /device:TPU:1 now
where the time goes in v1:
time: 508 us; the launch traced here: 507 us
  waiting for transfers between devices  311 us (61%)
  starting transfers between devices  118 us (23%)
  blocking collectives  24.3 us (5%)
  local copies, waits for them, and re-layouts  14.9 us (3%)
  other arithmetic  14.5 us (3%)
  between operations  14 us (3%)
  matrix products  10.1 us (2%)
    reduce_scatter x1, waiting for transfers between devices, local(): lax.psum_scatter(jnp.zeros((inv_rows * lax.axis_size('mesh'), CELLS), jnp...  237 us
    all_gather x1, waiting for transfers between devices, local(): gathered = lax.all_gather(log_sigma, 'mesh', axis=0, tiled=True)  68.6 us
    ppermute x11, starting transfers between devices, with_halo(): before = lax.ppermute(last, axis, up)  60.6 us
    ppermute x12, starting transfers between devices, from_partner(): return lax.ppermute(value, axis, pairs)  43.4 us
    all_gather x1, blocking collectives, local(): return jnp.sum(lax.all_gather(owned, ('group', 'comp')), axis=0)  24.3 us
    ppermute x11, starting transfers between devices, with_halo(): after = lax.ppermute(initial, axis, down)  14.1 us
  transfers between devices with their start and end apart: 36, of which 12 were waited for; matrix products, arithmetic and copies ran while one was open for 2% of the time, Pallas kernels for 0%

profile of v1, /device:TPU:1, one launch (start us, length us, event | category | flops | bytes accessed | tf_op | source)
XLA Modules:
  0.0 507.0 jit_solution(10799320339603767849)
XLA Ops:
  7.3 1.3 collective-permute-start.1
  8.6 4.6 collective-permute-start
  13.3 8.8 %collective-permute-start.2 = (f32[8,16384]{1,0:T(8,128)S(1)}, f32[8,16384]{1,0:T(8,128)S(1)}, u32[]{:S(2)}, u32[]{:S(2)}) collective-permute-start(f32[8,16384]{1,0:T(8,128)S(1)} %broadcast.154.clone), channel_id=1, source_target_pairs={{0,1},{1,0},{2,3},{3,2},{4,5},{5,4},{6,7},{7,6},{8,9},{9,8},{10,11... | collective-permute-start | bytes 1572872 | tf_op jit(solution)/shard_map/ppermute | solution.py:16
  22.1 1.2 gather_fusion.1
  25.3 68.6 %all-gather.3.cloned.1.call-done = f32[2048,128]{1,0:T(8,128)} async-done(((f32[64,128]{1,0:T(8,128)}), f32[2048,128]{1,0:T(8,128)}) %all-gather.3.cloned.1.call-update) | async-done | bytes 1048592 | tf_op jit(solution)/shard_map/all_gather | solution.py:66
  93.9 1.9 gather_fusion
  95.9 1.7 fusion.8
  97.5 7.0 %collective-permute-start.5 = (f32[8,16384]{1,0:T(8,128)S(1)}, f32[8,16384]{1,0:T(8,128)S(1)}, u32[]{:S(2)}, u32[]{:S(2)}) collective-permute-start(f32[8,16384]{1,0:T(8,128)S(1)} %fusion.8), channel_id=1, source_target_pairs={{0,1},{1,0},{2,3},{3,2},{4,5},{5,4},{6,7},{7,6},{8,9},{9,8},{10,11... | collective-permute-start | bytes 1572872 | tf_op jit(solution)/shard_map/ppermute | solution.py:16
  104.6 1.3 collective-permute-start.4
  105.9 4.0 collective-permute-start.3
  110.7 1.9 fusion.10
  112.6 3.1 collective-permute-start.8
  115.7 1.3 collective-permute-start.7
  117.0 4.5 collective-permute-start.6
  122.8 2.8 collective-permute-start.11
  125.7 1.3 collective-permute-start.10
  126.9 4.5 collective-permute-start.9
  132.2 0.9 fusion.14
  133.1 2.8 collective-permute-start.14
  136.0 1.3 collective-permute-start.13
  137.3 4.5 collective-permute-start.12
  143.1 2.8 collective-permute-start.17
  146.6 1.3 collective-permute-start.16
  147.9 5.2 %collective-permute-start.15 = (f32[8,1]{1,0:T(8,128)S(1)}, f32[8,1]{1,0:T(8,128)S(1)}, u32[]{:S(2)}, u32[]{:S(2)}) collective-permute-start(f32[8,1]{1,0:T(8,128)S(1)} %get-tuple-element.17), channel_id=1, source_target_pairs={{0,2},{2,4},{4,6},{6,8},{8,10},{10,12},{12,14},{14,16},{16,18},{18... | collective-permute-start | bytes 104 | tf_op jit(solution)/shard_map/ppermute | solution.py:26
  153.1 0.7 collective-permute-done.15
  153.9 1.9 fusion.18
  155.8 5.3 %copy.383 = f32[8,16384]{0,1:T(8,128)} copy(f32[8,16384]{1,0:T(8,128)S(1)} %fusion.18) | data formatting | bytes 1048576 | tf_op jit(solution)/shard_map/add | solution.py:56
  161.1 6.0 %scatter_custom_fusion = f32[8,16384]{0,1:T(8,128)} fusion(s32[128]{0:T(128)S(1)} %fusion.122, f32[]{:T(128)} %constant.12.clone.1, f32[1,1,8,128]{2,3,1,0:T(8,128)S(1)} %copy.384, f32[8,16384]{0,1:T(8,128)} %copy.383, s32[1024]{0:T(1024)S(1)} %pad_clamp_fusion), kind=kCustom, calls=%fused_computation.15 | custom fusion | flops 2048 | bytes 1118212 | tf_op jit(solution)/shard_map/scatter-add | solution.py:77
  167.1 5.5 %copy.385 = f32[8,16384]{1,0:T(8,128)S(1)} copy(f32[8,16384]{0,1:T(8,128)} %scatter_custom_fusion) | data formatting | bytes 1048576 | tf_op jit(solution)/shard_map/scatter-add | solution.py:77
  173.1 2.8 collective-permute-start.20
  175.9 1.3 collective-permute-start.19
  177.2 6.6 %collective-permute-start.18 = (f32[8,1]{1,0:T(8,128)S(1)}, f32[8,1]{1,0:T(8,128)S(1)}, u32[]{:S(2)}, u32[]{:S(2)}) collective-permute-start(f32[8,1]{1,0:T(8,128)S(1)} %get-tuple-element.15), channel_id=1, source_target_pairs={{0,2},{2,4},{4,6},{6,8},{8,10},{10,12},{12,14},{14,16},{16,18},{18... | collective-permute-start | bytes 104 | tf_op jit(solution)/shard_map/ppermute | solution.py:26
  185.2 2.8 collective-permute-start.23
  188.1 1.3 collective-permute-start.22
  189.4 6.6 %collective-permute-start.21 = (f32[8,1]{1,0:T(8,128)S(1)}, f32[8,1]{1,0:T(8,128)S(1)}, u32[]{:S(2)}, u32[]{:S(2)}) collective-permute-start(f32[8,1]{1,0:T(8,128)S(1)} %get-tuple-element.13), channel_id=1, source_target_pairs={{0,2},{2,4},{4,6},{6,8},{8,10},{10,12},{12,14},{14,16},{16,18},{18... | collective-permute-start | bytes 104 | tf_op jit(solution)/shard_map/ppermute | solution.py:26
  197.2 2.8 collective-permute-start.26
  200.0 1.3 collective-permute-start.25
  201.3 6.7 %collective-permute-start.24 = (f32[8,1]{1,0:T(8,128)S(1)}, f32[8,1]{1,0:T(8,128)S(1)}, u32[]{:S(2)}, u32[]{:S(2)}) collective-permute-start(f32[8,1]{1,0:T(8,128)S(1)} %get-tuple-element.11), channel_id=1, source_target_pairs={{0,2},{2,4},{4,6},{6,8},{8,10},{10,12},{12,14},{14,16},{16,18},{18... | collective-permute-start | bytes 104 | tf_op jit(solution)/shard_map/ppermute | solution.py:26
  209.4 2.8 collective-permute-start.29
  212.2 1.9 collective-permute-start.33
  214.2 1.3 collective-permute-start.28
  215.5 6.6 %collective-permute-start.27 = (f32[8,1]{1,0:T(8,128)S(1)}, f32[8,1]{1,0:T(8,128)S(1)}, u32[]{:S(2)}, u32[]{:S(2)}) collective-permute-start(f32[8,1]{1,0:T(8,128)S(1)} %get-tuple-element.9), channel_id=1, source_target_pairs={{0,2},{2,4},{4,6},{6,8},{8,10},{10,12},{12,14},{14,16},{16,18},{18... | collective-permute-start | bytes 104 | tf_op jit(solution)/shard_map/ppermute | solution.py:26
  223.3 3.3 collective-permute-start.32
  226.7 1.3 collective-permute-start.31
  227.9 6.6 %collective-permute-start.30 = (f32[8,1]{1,0:T(8,128)S(1)}, f32[8,1]{1,0:T(8,128)S(1)}, u32[]{:S(2)}, u32[]{:S(2)}) collective-permute-start(f32[8,1]{1,0:T(8,128)S(1)} %get-tuple-element.7), channel_id=1, source_target_pairs={{0,2},{2,4},{4,6},{6,8},{8,10},{10,12},{12,14},{14,16},{16,18},{18... | collective-permute-start | bytes 104 | tf_op jit(solution)/shard_map/ppermute | solution.py:26
  235.7 2.1 scatter_custom_fusion.1
  237.9 237.3 %reduce-scatter.2.cloned.1.call-done = f32[64,128]{1,0:T(8,128)} async-done(((f32[2048,128]{1,0:T(8,128)}), f32[64,128]{1,0:T(8,128)}) %reduce-scatter.2.cloned.1.call-update) | async-done | bytes 32784 | tf_op jit(solution)/shard_map/reduce_scatter | solution.py:83
  475.2 24.3 %all-gather = f32[1024,128]{1,0:T(8,128)S(1)} all-gather(f32[64,128]{1,0:T(8,128)} %reduce-scatter.2.cloned.1.call-done), channel_id=2, replica_groups=mesh['group'=8,'mesh'=32,'comp'=2] {'group','comp'}, dimensions={0}, use_global_device_ids=true | all-gather | bytes 557056 | tf_op jit(solution)/shard_map/all_gather | solution.py:91
  (83 shorter events, 15.5 us)
Async XLA Ops:
  6.5 15.5 %copy-start = (f32[128,128]{1,0:T(8,128)S(1)}, f32[128,128]{1,0:T(8,128)}, u32[]{:S(2)}) copy-start(f32[128,128]{1,0:T(8,128)} %param.10) | copy-start | bytes 196612
  6.5 115.8 %copy-start.1 = (f32[1,1,8,128,128]{4,3,2,1,0:T(8,128)S(1)}, f32[1,1,8,128,128]{4,3,2,1,0:T(8,128)}, u32[]{:S(2)}) copy-start(f32[1,1,8,128,128]{4,3,2,1,0:T(8,128)} %param.11) | copy-start | bytes 1572868
  6.5 87.3 %all-gather.3.cloned.1.call-start = ((), (), s32[]{:S(2)}) async-start(), calls=%async_computation.1 | async-start | bytes 1081344 | tf_op jit(solution)/shard_map/all_gather | solution.py:66
  7.3 467.9 %reduce-scatter.2.cloned.1.call-start = ((), (), s32[]{:S(2)}) async-start(), calls=%async_computation.2 | async-start | bytes 1081344 | tf_op jit(solution)/shard_map/reduce_scatter | solution.py:83
  7.3 88.5 %collective-permute-start.1 = (f32[8,1]{1,0:T(8,128)S(1)}, f32[8,1]{1,0:T(8,128)S(1)}, u32[]{:S(2)}, u32[]{:S(2)}) collective-permute-start(f32[8,1]{1,0:T(8,128)S(1)} %broadcast.157), channel_id=1, source_target_pairs={{2,0},{4,2},{6,4},{8,6},{10,8},{12,10},{14,12},{16,14},{18,16},{20... | collective-permute-start | bytes 104 | tf_op jit(solution)/shard_map/ppermute | solution.py:27
  8.6 87.2 %collective-permute-start = (f32[8,1]{1,0:T(8,128)S(1)}, f32[8,1]{1,0:T(8,128)S(1)}, u32[]{:S(2)}, u32[]{:S(2)}) collective-permute-start(f32[8,1]{1,0:T(8,128)S(1)} %broadcast.157), channel_id=1, source_target_pairs={{0,2},{2,4},{4,6},{6,8},{8,10},{10,12},{12,14},{14,16},{16,18},{18... | collective-permute-start | bytes 104 | tf_op jit(solution)/shard_map/ppermute | solution.py:26
  13.2 132.6 %copy-start.3 = (s32[1,128]{1,0:T(1,128)S(1)}, s32[1,128]{1,0:T(1,128)}, u32[]{:S(2)}) copy-start(s32[1,128]{1,0:T(1,128)} %param.12) | copy-start | bytes 1540
  13.3 132.6 %copy-start.2 = (f32[1,1,8,128]{3,2,1,0:T(8,128)S(1)}, f32[1,1,8,128]{3,2,1,0:T(8,128)}, u32[]{:S(2)}) copy-start(f32[1,1,8,128]{3,2,1,0:T(8,128)} %param.13) | copy-start | bytes 12292
  13.3 82.6 %collective-permute-start.2 = (f32[8,16384]{1,0:T(8,128)S(1)}, f32[8,16384]{1,0:T(8,128)S(1)}, u32[]{:S(2)}, u32[]{:S(2)}) collective-permute-start(f32[8,16384]{1,0:T(8,128)S(1)} %broadcast.154.clone), channel_id=1, source_target_pairs={{0,1},{1,0},{2,3},{3,2},{4,5},{5,4},{6,7},{7,6},{8,9},{9,8},{10,11... | collective-permute-start | bytes 1572872 | tf_op jit(solution)/shard_map/ppermute | solution.py:16
  97.5 13.1 %collective-permute-start.5 = (f32[8,16384]{1,0:T(8,128)S(1)}, f32[8,16384]{1,0:T(8,128)S(1)}, u32[]{:S(2)}, u32[]{:S(2)}) collective-permute-start(f32[8,16384]{1,0:T(8,128)S(1)} %fusion.8), channel_id=1, source_target_pairs={{0,1},{1,0},{2,3},{3,2},{4,5},{5,4},{6,7},{7,6},{8,9},{9,8},{10,11... | collective-permute-start | bytes 1572872 | tf_op jit(solution)/shard_map/ppermute | solution.py:16
  104.6 5.3 %collective-permute-start.4 = (f32[8,1]{1,0:T(8,128)S(1)}, f32[8,1]{1,0:T(8,128)S(1)}, u32[]{:S(2)}, u32[]{:S(2)}) collective-permute-start(f32[8,1]{1,0:T(8,128)S(1)} %get-tuple-element.26), channel_id=1, source_target_pairs={{2,0},{4,2},{6,4},{8,6},{10,8},{12,10},{14,12},{16,14},{18,16},{20... | collective-permute-start | bytes 104 | tf_op jit(solution)/shard_map/ppermute | solution.py:27
  105.9 4.7 collective-permute-start.3
  112.6 9.7 %collective-permute-start.8 = (f32[8,16384]{1,0:T(8,128)S(1)}, f32[8,16384]{1,0:T(8,128)S(1)}, u32[]{:S(2)}, u32[]{:S(2)}) collective-permute-start(f32[8,16384]{1,0:T(8,128)S(1)} %fusion.10), channel_id=1, source_target_pairs={{0,1},{1,0},{2,3},{3,2},{4,5},{5,4},{6,7},{7,6},{8,9},{9,8},{10,11... | collective-permute-start | bytes 1572872 | tf_op jit(solution)/shard_map/ppermute | solution.py:16
  115.7 6.4 %collective-permute-start.7 = (f32[8,1]{1,0:T(8,128)S(1)}, f32[8,1]{1,0:T(8,128)S(1)}, u32[]{:S(2)}, u32[]{:S(2)}) collective-permute-start(f32[8,1]{1,0:T(8,128)S(1)} %get-tuple-element.24), channel_id=1, source_target_pairs={{2,0},{4,2},{6,4},{8,6},{10,8},{12,10},{14,12},{16,14},{18,16},{20... | collective-permute-start | bytes 104 | tf_op jit(solution)/shard_map/ppermute | solution.py:27
  117.0 5.3 %collective-permute-start.6 = (f32[8,1]{1,0:T(8,128)S(1)}, f32[8,1]{1,0:T(8,128)S(1)}, u32[]{:S(2)}, u32[]{:S(2)}) collective-permute-start(f32[8,1]{1,0:T(8,128)S(1)} %get-tuple-element.23), channel_id=1, source_target_pairs={{0,2},{2,4},{4,6},{6,8},{8,10},{10,12},{12,14},{14,16},{16,18},{18... | collective-permute-start | bytes 104 | tf_op jit(solution)/shard_map/ppermute | solution.py:26
  122.8 9.4 %collective-permute-start.11 = (f32[8,16384]{1,0:T(8,128)S(1)}, f32[8,16384]{1,0:T(8,128)S(1)}, u32[]{:S(2)}, u32[]{:S(2)}) collective-permute-start(f32[8,16384]{1,0:T(8,128)S(1)} %fusion.12), channel_id=1, source_target_pairs={{0,1},{1,0},{2,3},{3,2},{4,5},{5,4},{6,7},{7,6},{8,9},{9,8},{10,11... | collective-permute-start | bytes 1572872 | tf_op jit(solution)/shard_map/ppermute | solution.py:16
  125.7 5.8 %collective-permute-start.10 = (f32[8,1]{1,0:T(8,128)S(1)}, f32[8,1]{1,0:T(8,128)S(1)}, u32[]{:S(2)}, u32[]{:S(2)}) collective-permute-start(f32[8,1]{1,0:T(8,128)S(1)} %get-tuple-element.22), channel_id=1, source_target_pairs={{2,0},{4,2},{6,4},{8,6},{10,8},{12,10},{14,12},{16,14},{18,16},{20... | collective-permute-start | bytes 104 | tf_op jit(solution)/shard_map/ppermute | solution.py:27
  126.9 5.3 %collective-permute-start.9 = (f32[8,1]{1,0:T(8,128)S(1)}, f32[8,1]{1,0:T(8,128)S(1)}, u32[]{:S(2)}, u32[]{:S(2)}) collective-permute-start(f32[8,1]{1,0:T(8,128)S(1)} %get-tuple-element.21), channel_id=1, source_target_pairs={{0,2},{2,4},{4,6},{6,8},{8,10},{10,12},{12,14},{14,16},{16,18},{18... | collective-permute-start | bytes 104 | tf_op jit(solution)/shard_map/ppermute | solution.py:26
  133.1 9.4 %collective-permute-start.14 = (f32[8,16384]{1,0:T(8,128)S(1)}, f32[8,16384]{1,0:T(8,128)S(1)}, u32[]{:S(2)}, u32[]{:S(2)}) collective-permute-start(f32[8,16384]{1,0:T(8,128)S(1)} %fusion.14), channel_id=1, source_target_pairs={{0,1},{1,0},{2,3},{3,2},{4,5},{5,4},{6,7},{7,6},{8,9},{9,8},{10,11... | collective-permute-start | bytes 1572872 | tf_op jit(solution)/shard_map/ppermute | solution.py:16
  136.0 6.4 %collective-permute-start.13 = (f32[8,1]{1,0:T(8,128)S(1)}, f32[8,1]{1,0:T(8,128)S(1)}, u32[]{:S(2)}, u32[]{:S(2)}) collective-permute-start(f32[8,1]{1,0:T(8,128)S(1)} %get-tuple-element.20), channel_id=1, source_target_pairs={{2,0},{4,2},{6,4},{8,6},{10,8},{12,10},{14,12},{16,14},{18,16},{20... | collective-permute-start | bytes 104 | tf_op jit(solution)/shard_map/ppermute | solution.py:27
  137.3 5.3 %collective-permute-start.12 = (f32[8,1]{1,0:T(8,128)S(1)}, f32[8,1]{1,0:T(8,128)S(1)}, u32[]{:S(2)}, u32[]{:S(2)}) collective-permute-start(f32[8,1]{1,0:T(8,128)S(1)} %get-tuple-element.19), channel_id=1, source_target_pairs={{0,2},{2,4},{4,6},{6,8},{8,10},{10,12},{12,14},{14,16},{16,18},{18... | collective-permute-start | bytes 104 | tf_op jit(solution)/shard_map/ppermute | solution.py:26
  143.1 10.8 %collective-permute-start.17 = (f32[8,16384]{1,0:T(8,128)S(1)}, f32[8,16384]{1,0:T(8,128)}, u32[]{:S(2)}, u32[]{:S(2)}) collective-permute-start(f32[8,16384]{1,0:T(8,128)S(1)} %fusion.16), channel_id=1, source_target_pairs={{0,1},{1,0},{2,3},{3,2},{4,5},{5,4},{6,7},{7,6},{8,9},{9,8},{10,11... | collective-permute-start | bytes 1572872 | tf_op jit(solution)/shard_map/ppermute | solution.py:16
  146.6 6.5 %collective-permute-start.16 = (f32[8,1]{1,0:T(8,128)S(1)}, f32[8,1]{1,0:T(8,128)S(1)}, u32[]{:S(2)}, u32[]{:S(2)}) collective-permute-start(f32[8,1]{1,0:T(8,128)S(1)} %get-tuple-element.18), channel_id=1, source_target_pairs={{2,0},{4,2},{6,4},{8,6},{10,8},{12,10},{14,12},{16,14},{18,16},{20... | collective-permute-start | bytes 104 | tf_op jit(solution)/shard_map/ppermute | solution.py:27
  147.9 5.9 %collective-permute-start.15 = (f32[8,1]{1,0:T(8,128)S(1)}, f32[8,1]{1,0:T(8,128)S(1)}, u32[]{:S(2)}, u32[]{:S(2)}) collective-permute-start(f32[8,1]{1,0:T(8,128)S(1)} %get-tuple-element.17), channel_id=1, source_target_pairs={{0,2},{2,4},{4,6},{6,8},{8,10},{10,12},{12,14},{14,16},{16,18},{18... | collective-permute-start | bytes 104 | tf_op jit(solution)/shard_map/ppermute | solution.py:26
  173.1 11.5 %collective-permute-start.20 = (f32[8,16384]{1,0:T(8,128)S(1)}, f32[8,16384]{1,0:T(8,128)S(1)}, u32[]{:S(2)}, u32[]{:S(2)}) collective-permute-start(f32[8,16384]{1,0:T(8,128)S(1)} %fusion.5), channel_id=1, source_target_pairs={{0,1},{1,0},{2,3},{3,2},{4,5},{5,4},{6,7},{7,6},{8,9},{9,8},{10,11... | collective-permute-start | bytes 1572872 | tf_op jit(solution)/shard_map/ppermute | solution.py:16
  175.9 7.9 %collective-permute-start.19 = (f32[8,1]{1,0:T(8,128)S(1)}, f32[8,1]{1,0:T(8,128)S(1)}, u32[]{:S(2)}, u32[]{:S(2)}) collective-permute-start(f32[8,1]{1,0:T(8,128)S(1)} %get-tuple-element.16), channel_id=1, source_target_pairs={{2,0},{4,2},{6,4},{8,6},{10,8},{12,10},{14,12},{16,14},{18,16},{20... | collective-permute-start | bytes 104 | tf_op jit(solution)/shard_map/ppermute | solution.py:27
  177.2 7.4 %collective-permute-start.18 = (f32[8,1]{1,0:T(8,128)S(1)}, f32[8,1]{1,0:T(8,128)S(1)}, u32[]{:S(2)}, u32[]{:S(2)}) collective-permute-start(f32[8,1]{1,0:T(8,128)S(1)} %get-tuple-element.15), channel_id=1, source_target_pairs={{0,2},{2,4},{4,6},{6,8},{8,10},{10,12},{12,14},{14,16},{16,18},{18... | collective-permute-start | bytes 104 | tf_op jit(solution)/shard_map/ppermute | solution.py:26
  185.2 11.5 %collective-permute-start.23 = (f32[8,16384]{1,0:T(8,128)S(1)}, f32[8,16384]{1,0:T(8,128)S(1)}, u32[]{:S(2)}, u32[]{:S(2)}) collective-permute-start(f32[8,16384]{1,0:T(8,128)S(1)} %fusion.50), channel_id=1, source_target_pairs={{0,1},{1,0},{2,3},{3,2},{4,5},{5,4},{6,7},{7,6},{8,9},{9,8},{10,11... | collective-permute-start | bytes 1572872 | tf_op jit(solution)/shard_map/ppermute | solution.py:16
  188.1 8.5 %collective-permute-start.22 = (f32[8,1]{1,0:T(8,128)S(1)}, f32[8,1]{1,0:T(8,128)S(1)}, u32[]{:S(2)}, u32[]{:S(2)}) collective-permute-start(f32[8,1]{1,0:T(8,128)S(1)} %get-tuple-element.14), channel_id=1, source_target_pairs={{2,0},{4,2},{6,4},{8,6},{10,8},{12,10},{14,12},{16,14},{18,16},{20... | collective-permute-start | bytes 104 | tf_op jit(solution)/shard_map/ppermute | solution.py:27
  189.4 7.4 %collective-permute-start.21 = (f32[8,1]{1,0:T(8,128)S(1)}, f32[8,1]{1,0:T(8,128)S(1)}, u32[]{:S(2)}, u32[]{:S(2)}) collective-permute-start(f32[8,1]{1,0:T(8,128)S(1)} %get-tuple-element.13), channel_id=1, source_target_pairs={{0,2},{2,4},{4,6},{6,8},{8,10},{10,12},{12,14},{14,16},{16,18},{18... | collective-permute-start | bytes 104 | tf_op jit(solution)/shard_map/ppermute | solution.py:26
  197.2 11.6 %collective-permute-start.26 = (f32[8,16384]{1,0:T(8,128)S(1)}, f32[8,16384]{1,0:T(8,128)S(1)}, u32[]{:S(2)}, u32[]{:S(2)}) collective-permute-start(f32[8,16384]{1,0:T(8,128)S(1)} %fusion.44), channel_id=1, source_target_pairs={{0,1},{1,0},{2,3},{3,2},{4,5},{5,4},{6,7},{7,6},{8,9},{9,8},{10,11... | collective-permute-start | bytes 1572872 | tf_op jit(solution)/shard_map/ppermute | solution.py:16
  200.0 8.0 %collective-permute-start.25 = (f32[8,1]{1,0:T(8,128)S(1)}, f32[8,1]{1,0:T(8,128)S(1)}, u32[]{:S(2)}, u32[]{:S(2)}) collective-permute-start(f32[8,1]{1,0:T(8,128)S(1)} %get-tuple-element.12), channel_id=1, source_target_pairs={{2,0},{4,2},{6,4},{8,6},{10,8},{12,10},{14,12},{16,14},{18,16},{20... | collective-permute-start | bytes 104 | tf_op jit(solution)/shard_map/ppermute | solution.py:27
  201.3 7.4 %collective-permute-start.24 = (f32[8,1]{1,0:T(8,128)S(1)}, f32[8,1]{1,0:T(8,128)S(1)}, u32[]{:S(2)}, u32[]{:S(2)}) collective-permute-start(f32[8,1]{1,0:T(8,128)S(1)} %get-tuple-element.11), channel_id=1, source_target_pairs={{0,2},{2,4},{4,6},{6,8},{8,10},{10,12},{12,14},{14,16},{16,18},{18... | collective-permute-start | bytes 104 | tf_op jit(solution)/shard_map/ppermute | solution.py:26
  209.4 13.5 %collective-permute-start.29 = (f32[8,16384]{1,0:T(8,128)S(1)}, f32[8,16384]{1,0:T(8,128)S(1)}, u32[]{:S(2)}, u32[]{:S(2)}) collective-permute-start(f32[8,16384]{1,0:T(8,128)S(1)} %fusion.38), channel_id=1, source_target_pairs={{0,1},{1,0},{2,3},{3,2},{4,5},{5,4},{6,7},{7,6},{8,9},{9,8},{10,11... | collective-permute-start | bytes 1572872 | tf_op jit(solution)/shard_map/ppermute | solution.py:16
  212.2 22.9 %collective-permute-start.33 = (f32[8,16384]{1,0:T(8,128)S(1)}, f32[8,16384]{1,0:T(8,128)S(1)}, u32[]{:S(2)}, u32[]{:S(2)}) collective-permute-start(f32[8,16384]{1,0:T(8,128)S(1)} %fusion.18), channel_id=1, source_target_pairs={{0,1},{1,0},{2,3},{3,2},{4,5},{5,4},{6,7},{7,6},{8,9},{9,8},{10,11... | collective-permute-start | bytes 1572872 | tf_op jit(solution)/shard_map/ppermute | solution.py:16
  214.2 8.5 %collective-permute-start.28 = (f32[8,1]{1,0:T(8,128)S(1)}, f32[8,1]{1,0:T(8,128)S(1)}, u32[]{:S(2)}, u32[]{:S(2)}) collective-permute-start(f32[8,1]{1,0:T(8,128)S(1)} %get-tuple-element.10), channel_id=1, source_target_pairs={{2,0},{4,2},{6,4},{8,6},{10,8},{12,10},{14,12},{16,14},{18,16},{20... | collective-permute-start | bytes 104 | tf_op jit(solution)/shard_map/ppermute | solution.py:27
  215.5 7.4 %collective-permute-start.27 = (f32[8,1]{1,0:T(8,128)S(1)}, f32[8,1]{1,0:T(8,128)S(1)}, u32[]{:S(2)}, u32[]{:S(2)}) collective-permute-start(f32[8,1]{1,0:T(8,128)S(1)} %get-tuple-element.9), channel_id=1, source_target_pairs={{0,2},{2,4},{4,6},{6,8},{8,10},{10,12},{12,14},{14,16},{16,18},{18... | collective-permute-start | bytes 104 | tf_op jit(solution)/shard_map/ppermute | solution.py:26
  223.3 12.0 %collective-permute-start.32 = (f32[8,16384]{1,0:T(8,128)S(1)}, f32[8,16384]{1,0:T(8,128)S(1)}, u32[]{:S(2)}, u32[]{:S(2)}) collective-permute-start(f32[8,16384]{1,0:T(8,128)S(1)} %fusion.32), channel_id=1, source_target_pairs={{0,1},{1,0},{2,3},{3,2},{4,5},{5,4},{6,7},{7,6},{8,9},{9,8},{10,11... | collective-permute-start | bytes 1572872 | tf_op jit(solution)/shard_map/ppermute | solution.py:16
  226.7 8.5 %collective-permute-start.31 = (f32[8,1]{1,0:T(8,128)S(1)}, f32[8,1]{1,0:T(8,128)S(1)}, u32[]{:S(2)}, u32[]{:S(2)}) collective-permute-start(f32[8,1]{1,0:T(8,128)S(1)} %get-tuple-element.8), channel_id=1, source_target_pairs={{2,0},{4,2},{6,4},{8,6},{10,8},{12,10},{14,12},{16,14},{18,16},{20... | collective-permute-start | bytes 104 | tf_op jit(solution)/shard_map/ppermute | solution.py:27
  227.9 7.4 %collective-permute-start.30 = (f32[8,1]{1,0:T(8,128)S(1)}, f32[8,1]{1,0:T(8,128)S(1)}, u32[]{:S(2)}, u32[]{:S(2)}) collective-permute-start(f32[8,1]{1,0:T(8,128)S(1)} %get-tuple-element.7), channel_id=1, source_target_pairs={{0,2},{2,4},{4,6},{6,8},{8,10},{10,12},{12,14},{14,16},{16,18},{18... | collective-permute-start | bytes 104 | tf_op jit(solution)/shard_map/ppermute | solution.py:26
Sparse Core Ops, SparseCore 0:
  10.5 83.2 all-gather.2
  238.0 237.1 reduce-scatter.1
